TPU v7x, 128 devices: a whole 4x4x4 slice. The times are simulated.
128 devices in a mesh: expert: 8 (over y, z_lo), fsdp: 16 (over x, z_hi, core).
Axes of the slice: x: 4, y: 4, z: 4 (z_hi: 2, z_lo: 2; z = z_hi * 2 + z_lo), core: 2. Of those that a mesh axis runs over, the one named last changes fastest.
Arguments:
- tokens: bfloat16 [18432, 2048], P(('expert', 'fsdp')), may hold values from -6 to 6
- expert_ids: int32 [18432, 6], P(('expert', 'fsdp')), may hold values from 0 to 15, as said below
- combine: float32 [18432, 6], P(('expert', 'fsdp')), may hold values from 0.05 to 1
- gate_weight: bfloat16 [16, 1408, 2048], P('expert', 'fsdp'), may hold values from -0.125 to 0.125
- up_weight: bfloat16 [16, 1408, 2048], P('expert', 'fsdp'), may hold values from -0.125 to 0.125
- down_weight: bfloat16 [16, 1408, 2048], P('expert', 'fsdp'), may hold values from -0.15625 to 0.15625
Outputs:
- mixed: bfloat16 [18432, 2048], P(('expert', 'fsdp'))
Inputs may be any that keep to these rules, and one draw needn't show every extreme that they name: `expert_ids`: each row names 6 different experts. Within the 144 rows of each device no expert is named more than 72 times, and one and the same expert is named exactly 72 times by the rows of every device.
All inputs are finite; a program needn't handle non-finite values.
Results may differ from a plain program's by a relative error of at most 0.0058.
Values may be sent and summed in bfloat16 or wider, within the bound.
A program may use at most 128 MiB of HBM per device.

v0:
```python
import jax
import jax.numpy as jnp
from jax import lax
from jax.sharding import PartitionSpec as P

CAP = 72


def add_piece(expert_rows, pieces):
    gate_piece, up_piece, down_piece = pieces
    gate_pre = jnp.einsum(
        "grd,gfd->grf", expert_rows, gate_piece, preferred_element_type=jnp.float32
    )
    up_pre = jnp.einsum("grd,gfd->grf", expert_rows, up_piece, preferred_element_type=jnp.float32)
    hidden = (jax.nn.silu(gate_pre) * up_pre).astype(jnp.bfloat16)
    return jnp.einsum("grf,gfd->grd", hidden, down_piece, preferred_element_type=jnp.float32)


def per_device(tokens, expert_ids, combine, gate_weight, up_weight, down_weight):
    groups = lax.axis_size("expert")
    per_group = gate_weight.shape[0]
    tok_rows, top_k = expert_ids.shape
    model_width = tokens.shape[1]
    flat_ids = expert_ids.reshape(-1)
    onehot = (flat_ids[:, None] == jnp.arange(per_group * groups, dtype=jnp.int32)[None, :]).astype(
        jnp.int32
    )
    earlier = jnp.cumsum(onehot, axis=0) - onehot
    rank_within = jnp.sum(earlier * onehot, axis=1)
    owner_group = flat_ids // per_group
    within = flat_ids % per_group
    slot_index = (within * groups + owner_group) * CAP + rank_within
    source = jnp.arange(tok_rows * top_k, dtype=jnp.int32) // top_k
    outgoing = (
        jnp.zeros((per_group * groups * CAP, model_width), jnp.bfloat16)
        .at[slot_index]
        .set(tokens[source])
    )
    outgoing = outgoing.reshape(per_group, groups, CAP, model_width)
    arrived = lax.all_to_all(outgoing, "expert", split_axis=1, concat_axis=1, tiled=True)
    expert_rows = arrived.reshape(per_group, groups * CAP, model_width)
    summed = add_piece(
        expert_rows,
        (
            lax.all_gather(gate_weight, "fsdp", axis=1, tiled=True),
            lax.all_gather(up_weight, "fsdp", axis=1, tiled=True),
            lax.all_gather(down_weight, "fsdp", axis=1, tiled=True),
        ),
    )
    produced = summed.astype(jnp.bfloat16)
    produced = produced.reshape(per_group, groups, CAP, model_width)
    returned = lax.all_to_all(produced, "expert", split_axis=1, concat_axis=1, tiled=True)
    back_rows = returned.reshape(per_group * groups * CAP, model_width)[slot_index]
    weighted = (
        back_rows.astype(jnp.float32).reshape(tok_rows, top_k, model_width) * combine[:, :, None]
    )
    return jnp.sum(weighted, axis=1).astype(jnp.bfloat16)


def solution(mesh):
    return jax.shard_map(
        per_device,
        mesh=mesh,
        in_specs=(
            P(("expert", "fsdp"), None),
            P(("expert", "fsdp"), None),
            P(("expert", "fsdp"), None),
            P("expert", "fsdp", None),
            P("expert", "fsdp", None),
            P("expert", "fsdp", None),
        ),
        out_specs=P(("expert", "fsdp"), None),
        check_vma=False,
    )
```

profile of v0, /device:TPU:1, one launch (start us, length us, event | category | flops | bytes accessed | tf_op | source)
XLA Modules:
  0.0 457.1 jit_solution(14942654767058175792)
XLA Ops:
  6.5 0.0 copy-start
  6.5 0.0 all-gather.4.cloned.1.call-start
  6.5 0.7 all-gather.4.cloned.1.call-update
  7.3 0.0 all-gather.6.cloned.1.call-start
  7.3 0.7 all-gather.6.cloned.1.call-update
  8.0 0.0 all-gather.8.cloned.1.call-start
  8.1 0.7 all-gather.8.cloned.1.call-update
  8.7 0.8 copy.21
  9.5 0.1 eq.24
  9.7 0.1 reshape.195
  9.9 2.0 reduce-window.6
  11.9 0.3 slice_reduce_fusion
  12.2 0.1 bitcast_bitcast_fusion
  12.4 0.0 copy-done
  12.4 23.2 %scatter_custom_fusion = bf16[1152,2048]{1,0:T(8,128)(2,1)} fusion(s32[864]{0:T(1024)S(1)} %fusion.5, bf16[144,2048]{1,0:T(8,128)(2,1)S(1)} %copy-done, s32[1024]{0:T(1024)S(1)} %pad_clamp_fusion.1, bf16[]{:T(256)} %constant.42.clone.1), kind=kCustom, calls=%fused_computation.6 | custom fusion | bytes 4718594 | tf_op jit(solution)/shard_map/scatter | solution.py:37
  35.6 2.8 copy.25
  38.4 66.5 %all_to_all.10 = bf16[2,8,72,2048]{3,2,0,1:T(8,128)(2,1)S(1)} all-to-all(bf16[2,8,72,2048]{3,2,0,1:T(8,128)(2,1)S(1)} %copy.25), channel_id=1, replica_groups=mesh['expert'=8,'fsdp'=16] {'expert'}, dimensions={1} | all-to-all | bytes 9437184 | tf_op jit(solution)/shard_map/all_to_all | solution.py:40
  104.9 2.5 copy.26
  107.4 38.9 %all-gather.4.cloned.1.call-done = bf16[2,1408,2048]{2,1,0:T(8,128)(2,1)} async-done(((bf16[2,88,2048]{2,1,0:T(8,128)(2,1)}), bf16[2,1408,2048]{2,1,0:T(8,128)(2,1)}) %all-gather.4.cloned.1.call-update) | async-done | bytes 11534352 | tf_op jit(solution)/shard_map/all_gather | solution.py:45
  146.3 14.4 %fusion.9 = f32[2,576,1408]{2,1,0:T(8,128)} fusion(bf16[2,576,2048]{2,1,0:T(8,128)(2,1)} %bitcast.33, bf16[2,1408,2048]{2,1,0:T(8,128)(2,1)} %all-gather.4.cloned.1.call-done), kind=kOutput, calls=%fused_computation.36 | convolution fusion | flops 6643777536 | bytes 22740992 | tf_op jit(solution)/shard_map/grd,gfd->grf/dot_general | solution.py:11
  160.7 71.9 %all-gather.6.cloned.1.call-done = bf16[2,1408,2048]{2,1,0:T(8,128)(2,1)} async-done(((bf16[2,88,2048]{2,1,0:T(8,128)(2,1)}), bf16[2,1408,2048]{2,1,0:T(8,128)(2,1)}) %all-gather.6.cloned.1.call-update) | async-done | bytes 11534352 | tf_op jit(solution)/shard_map/all_gather | solution.py:46
  232.6 86.3 %all-gather.8.cloned.1.call-done = bf16[2,1408,2048]{2,1,0:T(8,128)(2,1)} async-done(((bf16[2,88,2048]{2,1,0:T(8,128)(2,1)}), bf16[2,1408,2048]{2,1,0:T(8,128)(2,1)}) %all-gather.8.cloned.1.call-update) | async-done | bytes 11534352 | tf_op jit(solution)/shard_map/all_gather | solution.py:47
  318.8 22.8 %convolution_convert_fusion = bf16[2,576,2048]{2,1,0:T(8,128)(2,1)} fusion(bf16[2,1408,2048]{2,1,0:T(8,128)(2,1)} %all-gather.8.cloned.1.call-done, f32[2,576,1408]{2,1,0:T(8,128)} %fusion.9, bf16[2,576,2048]{2,1,0:T(8,128)(2,1)} %bitcast.34, bf16[2,1408,2048]{2,1,0:T(8,128)(2,1)} %all-gather.6.cloned.1.call-done), kind=kOutput, calls=%fused_computation.5 | convolution fusion | flops 13299646464 | bytes 38993920 | tf_op jit(solution)/shard_map/grf,gfd->grd/dot_general | solution.py:16
  341.6 5.2 %copy.27 = bf16[2,8,72,2048]{3,2,0,1:T(8,128)(2,1)} copy(bf16[2,8,72,2048]{3,2,1,0:T(8,128)(2,1)} %bitcast.35) | data formatting | bytes 9437184 | tf_op jit(solution)/shard_map/reshape | solution.py:51
  346.9 4.9 %all-to-all-start.1 = ((bf16[2,8,72,2048]{3,2,0,1:T(8,128)(2,1)}), bf16[2,8,72,2048]{3,2,0,1:T(8,128)(2,1)}, u32[]{:S(2)}, u32[]{:S(2)}) async-start(bf16[2,8,72,2048]{3,2,0,1:T(8,128)(2,1)} %copy.27), calls=%async_computation.1 | async-start | bytes 9437184 | tf_op jit(solution)/shard_map/all_to_all | solution.py:52
  351.8 0.0 copy-done.2
  351.8 0.1 copy.29
  351.9 66.3 %all-to-all-done.1 = bf16[2,8,72,2048]{3,2,0,1:T(8,128)(2,1)} async-done(((bf16[2,8,72,2048]{3,2,0,1:T(8,128)(2,1)}), bf16[2,8,72,2048]{3,2,0,1:T(8,128)(2,1)}, u32[]{:S(2)}, u32[]{:S(2)}) %all-to-all-start.1) | async-done | bytes 4718624 | tf_op jit(solution)/shard_map/all_to_all | solution.py:52
  418.2 5.2 %copy.28 = bf16[2,8,72,2048]{3,2,1,0:T(8,128)(2,1)} copy(bf16[2,8,72,2048]{3,2,0,1:T(8,128)(2,1)} %all-to-all-done.1) | data formatting | bytes 9437184 | tf_op jit(solution)/shard_map/all_to_all | solution.py:52
  423.5 11.7 %gather_fusion = bf16[864,2048]{1,0:T(8,128)(2,1)} fusion(bf16[1152,2048]{1,0:T(8,128)(2,1)} %bitcast.31, s32[1024]{0:T(1024)S(1)} %pad_clamp_fusion), kind=kCustom, calls=%fused_computation.1 | custom fusion | bytes 7081344 | tf_op jit(solution)/shard_map/gather | solution.py:53
  435.2 7.2 %reshape.203 = f32[144,6,2048]{2,1,0:T(8,128)} reshape(bf16[864,2048]{1,0:T(8,128)(2,1)} %gather_fusion) | data formatting | bytes 10616832 | tf_op jit(solution)/shard_map/convert_element_type | solution.py:55
  442.4 8.2 %multiply_reduce_fusion = bf16[144,2048]{1,0:T(8,128)(2,1)} fusion(f32[144,6,2048]{2,1,0:T(8,128)} %reshape.203, f32[144,6]{1,0:T(8,128)S(1)} %copy.29), kind=kLoop, calls=%fused_computation.3 | loop fusion | flops 3244032 | bytes 7671168 | tf_op jit(solution)/shard_map/reduce_sum | solution.py:57
  (11 shorter events, 0.2 us)
Async XLA Ops:
  6.5 5.9 %copy-start = (bf16[144,2048]{1,0:T(8,128)(2,1)S(1)}, bf16[144,2048]{1,0:T(8,128)(2,1)}, u32[]{:S(2)}) copy-start(bf16[144,2048]{1,0:T(8,128)(2,1)} %param.6) | copy-start | bytes 1769476
  6.5 139.8 %all-gather.4.cloned.1.call-start = ((), (), s32[]{:S(2)}) async-start(), calls=%async_computation.2 | async-start | bytes 12255232 | tf_op jit(solution)/shard_map/all_gather | solution.py:45
  7.3 225.3 %all-gather.6.cloned.1.call-start = ((), (), s32[]{:S(2)}) async-start(), calls=%async_computation.3 | async-start | bytes 12255232 | tf_op jit(solution)/shard_map/all_gather | solution.py:46
  8.0 310.8 %all-gather.8.cloned.1.call-start = ((), (), s32[]{:S(2)}) async-start(), calls=%async_computation.4 | async-start | bytes 12255232 | tf_op jit(solution)/shard_map/all_gather | solution.py:47
  346.9 5.0 %copy-start.2 = (f32[144,6]{0,1:T(8,128)S(1)}, f32[144,6]{0,1:T(8,128)}, u32[]{:S(2)}) copy-start(f32[144,6]{0,1:T(8,128)} %param.8) | copy-start | bytes 10372
  346.9 71.4 %all-to-all-start.1 = ((bf16[2,8,72,2048]{3,2,0,1:T(8,128)(2,1)}), bf16[2,8,72,2048]{3,2,0,1:T(8,128)(2,1)}, u32[]{:S(2)}, u32[]{:S(2)}) async-start(bf16[2,8,72,2048]{3,2,0,1:T(8,128)(2,1)} %copy.27), calls=%async_computation.1 | async-start | bytes 9437184 | tf_op jit(solution)/shard_map/all_to_all | solution.py:52
  435.2 15.4 %copy-start.1 = (bf16[144,2048]{1,0:T(8,128)(2,1)S(1)}, bf16[144,2048]{1,0:T(8,128)(2,1)}, u32[]{:S(2)}) copy-start(bf16[144,2048]{1,0:T(8,128)(2,1)} %param.6) | copy-start | bytes 1769476
Sparse Core Ops, SparseCore 0:
  9.8 136.4 all-gather.3
  148.8 83.7 all-gather.5
  235.1 83.7 all-gather.7
where the time goes:
time: 458 us; the launch traced here: 457 us
  waiting for transfers between devices  265 us (58%)
  blocking collectives  66.5 us (15%)
  local copies, waits for them, and re-layouts  59.3 us (13%)
  matrix products  37.2 us (8%)
  between operations  13.2 us (3%)
  other arithmetic  10.4 us (2%)
  starting transfers between devices  5.02 us (1%)
    all_gather x1, waiting for transfers between devices, per_device(): lax.all_gather(down_weight, 'fsdp', axis=1, tiled=True)  86.3 us
    all_gather x1, waiting for transfers between devices, per_device(): lax.all_gather(up_weight, 'fsdp', axis=1, tiled=True)  71.9 us
    all_to_all x1, blocking collectives, per_device(): lax.all_to_all(outgoing, 'expert', split_axis=1, concat_axis=1, tiled=True)  66.5 us
    all_to_all x1, waiting for transfers between devices, per_device(): lax.all_to_all(produced, 'expert', split_axis=1, concat_axis=1, tiled=True)  66.3 us
    all_gather x1, waiting for transfers between devices, per_device(): lax.all_gather(gate_weight, 'fsdp', axis=1, tiled=True)  38.9 us
    scatter x1, local copies, waits for them, and re-layouts, per_device(): outgoing = jnp.zeros((per_group * groups * CAP, model_width), jnp.bfloat1...  23.2 us
    dot_general x1, matrix products, add_piece(): jnp.einsum('grf,gfd->grd', hidden, down_piece, preferred_element_type=jnp...  22.8 us
    dot_general x1, matrix products, add_piece(): jnp.einsum('grd,gfd->grf', expert_rows, gate_piece, preferred_element_typ...  14.4 us
  transfers between devices with their start and end apart: 4, of which 4 were waited for; matrix products, arithmetic and copies ran while one was open for 10% of the time, Pallas kernels for 0%

commit v1 on v0

--- a/solution.py
+++ b/solution.py
@@ -39,12 +39,15 @@
     outgoing = outgoing.reshape(per_group, groups, CAP, model_width)
     arrived = lax.all_to_all(outgoing, "expert", split_axis=1, concat_axis=1, tiled=True)
     expert_rows = arrived.reshape(per_group, groups * CAP, model_width)
+    return_all_sectors = lambda chip_axis, values: jnp.concatenate(
+        lax.all_to_all(jnp.stack(lax.psum(1, chip_axis) * [values]), chip_axis, 0, 0), 1
+    )
     summed = add_piece(
         expert_rows,
         (
             lax.all_gather(gate_weight, "fsdp", axis=1, tiled=True),
             lax.all_gather(up_weight, "fsdp", axis=1, tiled=True),
-            lax.all_gather(down_weight, "fsdp", axis=1, tiled=True),
+            return_all_sectors("fsdp", down_weight),
         ),
     )
     produced = summed.astype(jnp.bfloat16)

time: 458 us -> 505 us (1.10)
  the two profiles are of different devices: /device:TPU:1 before, /device:TPU:66 now
where the time goes in v1:
time: 505 us; the launch traced here: 504 us
  waiting for transfers between devices  283 us (56%)
  local copies, waits for them, and re-layouts  77.6 us (15%)
  blocking collectives  69.8 us (14%)
  matrix products  37.1 us (7%)
  between operations  13.5 us (3%)
  starting transfers between devices  12.2 us (2%)
  other arithmetic  10.4 us (2%)
    all_to_all x1, waiting for transfers between devices, per_device(): lax.all_to_all(jnp.stack(lax.psum(1, chip_axis) * [values]), chip_axis, 0...  150 us
    all_to_all x1, blocking collectives, per_device(): lax.all_to_all(outgoing, 'expert', split_axis=1, concat_axis=1, tiled=True)  69.8 us
    all_to_all x1, waiting for transfers between devices, per_device(): lax.all_to_all(produced, 'expert', split_axis=1, concat_axis=1, tiled=True)  67.1 us
    all_gather x1, waiting for transfers between devices, per_device(): lax.all_gather(up_weight, 'fsdp', axis=1, tiled=True)  64.8 us
    scatter x1, local copies, waits for them, and re-layouts, per_device(): outgoing = jnp.zeros((per_group * groups * CAP, model_width), jnp.bfloat1...  23.2 us
    dot_general x1, matrix products, add_piece(): jnp.einsum('grf,gfd->grd', hidden, down_piece, preferred_element_type=jnp...  22.8 us
    dot_general x1, matrix products, add_piece(): jnp.einsum('grd,gfd->grf', expert_rows, gate_piece, preferred_element_typ...  14.4 us
    gather x1, local copies, waits for them, and re-layouts, per_device(): returned.reshape(per_group * groups * CAP, model_width)[slot_index]  11.7 us
  transfers between devices with their start and end apart: 4, of which 3 were waited for; matrix products, arithmetic and copies ran while one was open for 13% of the time, Pallas kernels for 0%

profile of v1, /device:TPU:66, one launch (start us, length us, event | category | flops | bytes accessed | tf_op | source)
XLA Modules:
  0.0 503.7 jit_solution(2212052876440020318)
XLA Ops:
  6.5 0.0 copy-start
  6.5 0.7 all-gather.3.cloned.1.call-update
  7.3 0.0 all-gather.5.cloned.1.call-start
  7.3 0.7 all-gather.5.cloned.1.call-update
  8.0 0.8 copy.22
  8.8 0.1 eq.24
  9.0 0.1 reshape.203
  9.1 2.0 reduce-window.6
  11.1 0.3 slice_reduce_fusion
  11.5 0.1 bitcast_bitcast_fusion
  11.7 23.2 %scatter_custom_fusion = bf16[1152,2048]{1,0:T(8,128)(2,1)} fusion(s32[864]{0:T(1024)S(1)} %fusion.5, bf16[144,2048]{1,0:T(8,128)(2,1)S(1)} %copy-done, s32[1024]{0:T(1024)S(1)} %pad_clamp_fusion.1, bf16[]{:T(256)} %constant.42.clone.1), kind=kCustom, calls=%fused_computation.6 | custom fusion | bytes 4718594 | tf_op jit(solution)/shard_map/scatter | solution.py:37
  34.9 2.7 copy.26
  37.6 0.0 copy-start.2
  37.6 69.8 %all_to_all.15 = bf16[2,8,72,2048]{3,2,0,1:T(8,128)(2,1)} all-to-all(bf16[2,8,72,2048]{3,2,0,1:T(8,128)(2,1)S(1)} %copy.26), channel_id=1, replica_groups=mesh['expert'=8,'fsdp'=16] {'expert'}, dimensions={1} | all-to-all | bytes 9437184 | tf_op jit(solution)/shard_map/all_to_all | solution.py:40
  107.4 5.7 %stack.2 = bf16[16,2,88,2048]{3,2,1,0:T(8,128)(2,1)} broadcast(bf16[2,88,2048]{2,1,0:T(8,128)(2,1)S(1)} %copy-done.2), dimensions={1,2,3} | broadcast | bytes 12255232 | tf_op jit(solution)/shard_map/stack | solution.py:43
  113.1 7.3 %all-to-all-start.1 = ((bf16[16,2,88,2048]{3,2,1,0:T(8,128)(2,1)}), bf16[16,2,88,2048]{3,2,1,0:T(8,128)(2,1)}, u32[]{:S(2)}, u32[]{:S(2)}) async-start(bf16[16,2,88,2048]{3,2,1,0:T(8,128)(2,1)} %stack.2), calls=%async_computation.1 | async-start | bytes 23068672 | tf_op jit(solution)/shard_map/all_to_all | solution.py:43
  120.3 5.2 %copy.27 = bf16[2,8,72,2048]{3,2,1,0:T(8,128)(2,1)} copy(bf16[2,8,72,2048]{3,2,0,1:T(8,128)(2,1)} %all_to_all.15) | data formatting | bytes 9437184 | tf_op jit(solution)/shard_map/all_to_all | solution.py:40
  125.5 149.7 %all-to-all-done.1 = bf16[16,2,88,2048]{3,2,1,0:T(8,128)(2,1)} async-done(((bf16[16,2,88,2048]{3,2,1,0:T(8,128)(2,1)}), bf16[16,2,88,2048]{3,2,1,0:T(8,128)(2,1)}, u32[]{:S(2)}, u32[]{:S(2)}) %all-to-all-start.1) | async-done | bytes 11534368 | tf_op jit(solution)/shard_map/all_to_all | solution.py:43
  275.2 9.9 %copy.28 = bf16[2,16,88,2048]{3,2,1,0:T(8,128)(2,1)} copy(bf16[2,16,88,2048]{3,2,0,1:T(8,128)(2,1)} %bitcast.3) | data formatting | bytes 23068672 | tf_op jit(solution)/shard_map/reshape | solution.py:42
  285.2 14.4 %fusion.9 = f32[2,576,1408]{2,1,0:T(8,128)} fusion(bf16[2,576,2048]{2,1,0:T(8,128)(2,1)} %bitcast.36, bf16[2,1408,2048]{2,1,0:T(8,128)(2,1)} %all-gather.3.cloned.1.call-done), kind=kOutput, calls=%fused_computation.36 | convolution fusion | flops 6643777536 | bytes 22740992 | tf_op jit(solution)/shard_map/grd,gfd->grf/dot_general | solution.py:11
  299.6 64.8 %all-gather.5.cloned.1.call-done = bf16[2,1408,2048]{2,1,0:T(8,128)(2,1)} async-done(((bf16[2,88,2048]{2,1,0:T(8,128)(2,1)}), bf16[2,1408,2048]{2,1,0:T(8,128)(2,1)}) %all-gather.5.cloned.1.call-update) | async-done | bytes 11534352 | tf_op jit(solution)/shard_map/all_gather | solution.py:49
  364.4 22.8 %convolution_convert_fusion = bf16[2,576,2048]{2,1,0:T(8,128)(2,1)} fusion(bf16[2,1408,2048]{2,1,0:T(8,128)(2,1)} %bitcast.35, f32[2,576,1408]{2,1,0:T(8,128)} %fusion.9, bf16[2,576,2048]{2,1,0:T(8,128)(2,1)} %bitcast.37, bf16[2,1408,2048]{2,1,0:T(8,128)(2,1)} %all-gather.5.cloned.1.call-done), kind=kOutput, calls=%fused_computation.5 | convolution fusion | flops 13299646464 | bytes 38993920 | tf_op jit(solution)/shard_map/grf,gfd->grd/dot_general | solution.py:16
  387.1 5.2 %copy.29 = bf16[2,8,72,2048]{3,2,0,1:T(8,128)(2,1)} copy(bf16[2,8,72,2048]{3,2,1,0:T(8,128)(2,1)} %bitcast.38) | data formatting | bytes 9437184 | tf_op jit(solution)/shard_map/reshape | solution.py:54
  392.4 4.9 all-to-all-start.2
  397.3 0.0 copy-done.3
  397.3 0.1 copy.31
  397.4 67.1 %all-to-all-done.2 = bf16[2,8,72,2048]{3,2,0,1:T(8,128)(2,1)} async-done(((bf16[2,8,72,2048]{3,2,0,1:T(8,128)(2,1)}), bf16[2,8,72,2048]{3,2,0,1:T(8,128)(2,1)}, u32[]{:S(2)}, u32[]{:S(2)}) %all-to-all-start.2) | async-done | bytes 4718624 | tf_op jit(solution)/shard_map/all_to_all | solution.py:55
  464.6 5.2 %copy.30 = bf16[2,8,72,2048]{3,2,1,0:T(8,128)(2,1)} copy(bf16[2,8,72,2048]{3,2,0,1:T(8,128)(2,1)} %all-to-all-done.2) | data formatting | bytes 9437184 | tf_op jit(solution)/shard_map/all_to_all | solution.py:55
  469.8 11.7 %gather_fusion = bf16[864,2048]{1,0:T(8,128)(2,1)} fusion(bf16[1152,2048]{1,0:T(8,128)(2,1)} %bitcast.33, s32[1024]{0:T(1024)S(1)} %pad_clamp_fusion), kind=kCustom, calls=%fused_computation.1 | custom fusion | bytes 7081344 | tf_op jit(solution)/shard_map/gather | solution.py:56
  481.5 7.2 %reshape.213 = f32[144,6,2048]{2,1,0:T(8,128)} reshape(bf16[864,2048]{1,0:T(8,128)(2,1)} %gather_fusion) | data formatting | bytes 10616832 | tf_op jit(solution)/shard_map/convert_element_type | solution.py:58
  488.7 8.2 %multiply_reduce_fusion = bf16[144,2048]{1,0:T(8,128)(2,1)} fusion(f32[144,6,2048]{2,1,0:T(8,128)} %reshape.213, f32[144,6]{1,0:T(8,128)S(1)} %copy.31), kind=kLoop, calls=%fused_computation.3 | loop fusion | flops 3244032 | bytes 7671168 | tf_op jit(solution)/shard_map/reduce_sum | solution.py:60
  496.9 0.0 copy-done.1
  (14 shorter events, 0.2 us)
Async XLA Ops:
  6.5 5.1 %copy-start = (bf16[144,2048]{1,0:T(8,128)(2,1)S(1)}, bf16[144,2048]{1,0:T(8,128)(2,1)}, u32[]{:S(2)}) copy-start(bf16[144,2048]{1,0:T(8,128)(2,1)} %param.6) | copy-start | bytes 1769476
  6.5 278.6 %all-gather.3.cloned.1.call-start = ((), (), s32[]{:S(2)}) async-start(), calls=%async_computation.3 | async-start | bytes 12255232 | tf_op jit(solution)/shard_map/all_gather | solution.py:48
  7.3 357.1 %all-gather.5.cloned.1.call-start = ((), (), s32[]{:S(2)}) async-start(), calls=%async_computation.4 | async-start | bytes 12255232 | tf_op jit(solution)/shard_map/all_gather | solution.py:49
  37.6 69.8 %copy-start.2 = (bf16[2,88,2048]{2,1,0:T(8,128)(2,1)S(1)}, bf16[2,88,2048]{2,1,0:T(8,128)(2,1)}, u32[]{:S(2)}) copy-start(bf16[2,88,2048]{2,1,0:T(8,128)(2,1)} %param.11) | copy-start | bytes 2162692
  113.1 162.2 %all-to-all-start.1 = ((bf16[16,2,88,2048]{3,2,1,0:T(8,128)(2,1)}), bf16[16,2,88,2048]{3,2,1,0:T(8,128)(2,1)}, u32[]{:S(2)}, u32[]{:S(2)}) async-start(bf16[16,2,88,2048]{3,2,1,0:T(8,128)(2,1)} %stack.2), calls=%async_computation.1 | async-start | bytes 23068672 | tf_op jit(solution)/shard_map/all_to_all | solution.py:43
  392.4 5.0 copy-start.3
  392.4 72.2 %all-to-all-start.2 = ((bf16[2,8,72,2048]{3,2,0,1:T(8,128)(2,1)}), bf16[2,8,72,2048]{3,2,0,1:T(8,128)(2,1)}, u32[]{:S(2)}, u32[]{:S(2)}) async-start(bf16[2,8,72,2048]{3,2,0,1:T(8,128)(2,1)} %copy.29), calls=%async_computation.2 | async-start | bytes 9437184 | tf_op jit(solution)/shard_map/all_to_all | solution.py:55
  481.5 15.4 %copy-start.1 = (bf16[144,2048]{1,0:T(8,128)(2,1)S(1)}, bf16[144,2048]{1,0:T(8,128)(2,1)}, u32[]{:S(2)}) copy-start(bf16[144,2048]{1,0:T(8,128)(2,1)} %param.6) | copy-start | bytes 1769476
Sparse Core Ops, SparseCore 0:
  9.8 169.4 all-gather.2
  181.8 182.5 all-gather.4
